TPU v7x, 128 devices: a whole 4x4x4 slice. The times are simulated.
128 devices in a mesh: blk: 4 (over x_lo, core), inner: 32 (over y, x_hi, z).
Axes of the slice: x: 4 (x_hi: 2, x_lo: 2; x = x_hi * 2 + x_lo), y: 4, z: 4, core: 2. Of those that a mesh axis runs over, the one named last changes fastest.
Arguments:
- queries: bfloat16 [32768, 4096], P(('blk', 'inner')), may hold values from -5 to 5
- keys: bfloat16 [32768, 512], P(('blk', 'inner')), may hold values from -5 to 5
- values: bfloat16 [32768, 512], P(('blk', 'inner')), may hold values from -6 to 6
- out_grad: bfloat16 [32768, 4096], P(('blk', 'inner')), may hold values from -6 to 6
- doc_lengths: int32 [64], replicated, may hold values from 1 to 768, 32768 in all
Outputs:
- attended: bfloat16 [32768, 4096], P(('blk', 'inner'))
- query_grad: bfloat16 [32768, 4096], P(('blk', 'inner'))
- key_grad: bfloat16 [32768, 512], P(('blk', 'inner'))
- value_grad: bfloat16 [32768, 512], P(('blk', 'inner'))
All inputs are finite; a program needn't handle non-finite values.
Results may differ from a plain program's by a relative error of at most 0.025.
Values may be sent and summed in bfloat16 or wider, within the bound.
A program may use at most 128 MiB of HBM per device.

v0:
```python
import math

import jax
import jax.numpy as jnp
from jax import lax
from jax.experimental import pallas as pl
from jax.experimental.pallas import tpu as pltpu
from jax.sharding import PartitionSpec as P

HEAD = 128
KV_HEADS = 4
GROUP = 8
SPAN = 4
SUB = 128
MESH = pl.DeviceIdType.MESH
NT = (((1,), (1,)), ((), ()))
NN = (((1,), (0,)), ((), ()))


def dot(a, b, dims):
    return lax.dot_general(a, b, dims, preferred_element_type=jnp.float32)


def fold_rows(x, op):
    rows = x.shape[0]
    parts = [x[r : r + 8] for r in range(0, rows, 8)]
    while len(parts) > 1:
        parts = [op(parts[i], parts[i + 1]) for i in range(0, len(parts), 2)]
    return parts[0]


def kernel(
    q_hbm,
    k_hbm,
    v_hbm,
    g_hbm,
    len_ref,
    att_ref,
    dq_ref,
    dk_ref,
    dv_ref,
    q_v,
    g_v,
    win,
    win_t,
    bias,
    s_ref,
    dp_ref,
    w_ref,
    ds_ref,
    acc,
    own,
    out_part,
    in_part,
    load_sem,
    own_sem,
    send_sem,
    recv_sem,
    back_send,
    back_recv,
):
    T = q_hbm.shape[0]
    W = SPAN * T
    WIN = W - SUB
    inner = lax.axis_size("inner")
    count = lax.axis_size("blk") * inner
    me = lax.axis_index("blk") * inner + lax.axis_index("inner")
    scale = 1.0 / math.sqrt(HEAD)
    cols = GROUP * HEAD

    def device(offset):
        there = lax.rem(me + offset + count, count)
        return (there // inner, lax.rem(there, inner))

    def load(j, which):
        src, dst = ((q_hbm, q_v), (g_hbm, g_v))[which]
        at = pl.ds(pl.multiple_of(j * cols, cols), cols)
        return pltpu.make_async_copy(src.at[:, at], dst.at[j], load_sem.at[j, which])

    def own_copy(j, which):
        src = (k_hbm, v_hbm)[which]
        at = pl.ds(pl.multiple_of(j * HEAD, HEAD), HEAD)
        return pltpu.make_async_copy(
            src.at[:, at], win.at[which, j, pl.ds(W - T, T), :], own_sem.at[j, which]
        )

    def send(j, d, which):
        src = (k_hbm, v_hbm)[which]
        at = pl.ds(pl.multiple_of(j * HEAD, HEAD), HEAD)
        return pltpu.make_async_remote_copy(
            src_ref=src.at[:, at],
            dst_ref=win.at[which, j, pl.ds((SPAN - 1 - d) * T, T), :],
            send_sem=send_sem.at[j, d - 1, which],
            recv_sem=recv_sem.at[j, d - 1, which],
            device_id=device(d),
            device_id_type=MESH,
        )

    def back(j, d, which):
        return pltpu.make_async_remote_copy(
            src_ref=out_part.at[which, j, pl.ds((SPAN - 1 - d) * T, T), :],
            dst_ref=in_part.at[which, j, d - 1],
            send_sem=back_send.at[j, d - 1, which],
            recv_sem=back_recv.at[j, d - 1, which],
            device_id=device(-d),
            device_id_type=MESH,
        )

    def each(fn):
        for d in range(1, SPAN):
            for which in range(2):
                fn(d, which)

    barrier = pltpu.get_barrier_semaphore()
    for d in range(1, SPAN):
        for sign in (1, -1):
            pl.semaphore_signal(barrier, inc=1, device_id=device(sign * d), device_id_type=MESH)

    @pl.loop(0, KV_HEADS)
    def _(j):
        for which in range(2):
            own_copy(j, which).start()
            load(j, which).start()

    pl.semaphore_wait(barrier, 2 * (SPAN - 1))
    each(lambda d, which: send(0, d, which).start())

    q_pos = me * T + lax.broadcasted_iota(jnp.int32, (8, T), 1)

    def doc_step(i, carry):
        end, first = carry
        end = end + len_ref[i]
        return end, jnp.where(q_pos >= end, end, first)

    _, first = lax.fori_loop(
        0, len_ref.shape[0], doc_step, (jnp.int32(0), jnp.zeros((8, T), jnp.int32))
    )
    for sub in range(T // SUB):
        low = first[0:1, sub * SUB : (sub + 1) * SUB]
        high = q_pos[0:1, sub * SUB : (sub + 1) * SUB]
        start = (me - (SPAN - 1)) * T + sub * SUB
        for c in range(WIN // SUB):
            k_pos = start + c * SUB + lax.broadcasted_iota(jnp.int32, (SUB, SUB), 0)
            ok = (k_pos >= low) & (k_pos <= high)
            bias[sub, c * SUB : (c + 1) * SUB, :] = jnp.where(ok, 0.0, -1e30)

    @pl.loop(0, KV_HEADS)
    def _(j):
        @pl.when(j + 1 < KV_HEADS)
        def _():
            each(lambda d, which: send(j + 1, d, which).start())

        for which in range(2):
            own_copy(j, which).wait()
            load(j, which).wait()
        each(lambda d, which: send(j, d, which).wait_recv())
        for which in range(2):
            for r in range(0, W, SUB):
                win_t[which, :, r : r + SUB] = win[which, j, r : r + SUB, :].T
        acc[...] = jnp.zeros_like(acc)

        def unit(pair, sub):
            rows = slice(sub * SUB, (sub + 1) * SUB)
            col0 = pl.ds(pl.multiple_of(pair * 2 * HEAD, HEAD), HEAD)
            col1 = pl.ds(pl.multiple_of(pair * 2 * HEAD + HEAD, HEAD), HEAD)
            out0 = pl.ds(pl.multiple_of(j * cols + pair * 2 * HEAD, HEAD), HEAD)
            out1 = pl.ds(pl.multiple_of(j * cols + pair * 2 * HEAD + HEAD, HEAD), HEAD)
            qu = jnp.concatenate([q_v[j, rows, col0], q_v[j, rows, col1]], axis=0)
            gu = jnp.concatenate([g_v[j, rows, col0], g_v[j, rows, col1]], axis=0)

            def keys(c):
                return slice((sub + c) * SUB, (sub + c + 1) * SUB)

            top = None
            for c in range(WIN // SUB):
                at = slice(c * SUB, (c + 1) * SUB)
                extra = bias[sub, at, :]
                s = dot(win[0, j, keys(c), :], qu, NT) + jnp.concatenate([extra, extra], axis=1)
                s_ref[at, :] = s
                part = fold_rows(s, jnp.maximum)
                top = part if top is None else jnp.maximum(top, part)
            top = jnp.max(top, axis=0, keepdims=True)
            total = jnp.zeros((8, 2 * SUB), jnp.float32)
            cross = jnp.zeros((8, 2 * SUB), jnp.float32)
            for c in range(WIN // SUB):
                at = slice(c * SUB, (c + 1) * SUB)
                p = jnp.exp2((s_ref[at, :] - top) * (scale * math.log2(math.e)))
                dp = dot(win[1, j, keys(c), :], gu, NT)
                total = total + fold_rows(p, jnp.add)
                cross = cross + fold_rows(p * dp, jnp.add)
                s_ref[at, :] = p
                dp_ref[at, :] = dp
            inv = 1.0 / jnp.sum(total, axis=0, keepdims=True)
            delta = jnp.sum(cross, axis=0, keepdims=True) * inv
            for c in range(WIN // SUB):
                at = slice(c * SUB, (c + 1) * SUB)
                w = s_ref[at, :] * inv
                w_ref[at, :] = w.astype(jnp.bfloat16)
                ds_ref[at, :] = (w * (dp_ref[at, :] - delta)).astype(jnp.bfloat16)
            span = slice(sub * SUB, sub * SUB + WIN)
            o_t = dot(win_t[1, :, span], w_ref[...], NN)
            dq_t = dot(win_t[0, :, span], ds_ref[...], NN) * scale
            att_ref[rows, out0] = o_t[:, :SUB].T.astype(jnp.bfloat16)
            att_ref[rows, out1] = o_t[:, SUB:].T.astype(jnp.bfloat16)
            dq_ref[rows, out0] = dq_t[:, :SUB].T.astype(jnp.bfloat16)
            dq_ref[rows, out1] = dq_t[:, SUB:].T.astype(jnp.bfloat16)
            acc[0, span, :] += dot(ds_ref[...], qu, NN)
            acc[1, span, :] += dot(w_ref[...], gu, NN)

        @pl.loop(0, GROUP // 2)
        def _(pair):
            for sub in range(T // SUB):
                unit(pair, sub)

        for which in range(2):
            factor = scale if which == 0 else 1.0
            out_part[which, j] = (acc[which, : W - T, :] * factor).astype(jnp.bfloat16)
            own[which, j] = acc[which, W - T :, :] * factor
        each(lambda d, which: back(j, d, which).start())

    @pl.loop(0, KV_HEADS)
    def _(j):
        each(lambda d, which: back(j, d, which).wait_recv())
        at = pl.ds(pl.multiple_of(j * HEAD, HEAD), HEAD)
        for which, ref in ((0, dk_ref), (1, dv_ref)):
            sums = own[which, j]
            for d in range(1, SPAN):
                sums = sums + in_part[which, j, d - 1].astype(jnp.float32)
            ref[:, at] = sums.astype(jnp.bfloat16)

    @pl.loop(0, KV_HEADS)
    def _(j):
        each(lambda d, which: send(j, d, which).wait_send())
        each(lambda d, which: back(j, d, which).wait_send())


def local(queries, keys, values, out_grad, doc_lengths):
    T = queries.shape[0]
    W = SPAN * T
    WIN = W - SUB
    bf16, f32 = jnp.bfloat16, jnp.float32
    anywhere = pl.BlockSpec(memory_space=pl.ANY)
    vmem = pl.BlockSpec(memory_space=pltpu.VMEM)
    dma = pltpu.SemaphoreType.DMA
    return pl.pallas_call(
        kernel,
        out_shape=(
            jax.ShapeDtypeStruct(queries.shape, bf16),
            jax.ShapeDtypeStruct(queries.shape, bf16),
            jax.ShapeDtypeStruct(keys.shape, bf16),
            jax.ShapeDtypeStruct(keys.shape, bf16),
        ),
        in_specs=[anywhere] * 4 + [pl.BlockSpec(memory_space=pltpu.SMEM)],
        out_specs=(vmem, vmem, vmem, vmem),
        scratch_shapes=[
            pltpu.VMEM((KV_HEADS, T, GROUP * HEAD), bf16),
            pltpu.VMEM((KV_HEADS, T, GROUP * HEAD), bf16),
            pltpu.VMEM((2, KV_HEADS, W, HEAD), bf16),
            pltpu.VMEM((2, HEAD, W), bf16),
            pltpu.VMEM((T // SUB, WIN, SUB), f32),
            pltpu.VMEM((WIN, 2 * SUB), f32),
            pltpu.VMEM((WIN, 2 * SUB), f32),
            pltpu.VMEM((WIN, 2 * SUB), bf16),
            pltpu.VMEM((WIN, 2 * SUB), bf16),
            pltpu.VMEM((2, W, HEAD), f32),
            pltpu.VMEM((2, KV_HEADS, T, HEAD), f32),
            pltpu.VMEM((2, KV_HEADS, W - T, HEAD), bf16),
            pltpu.VMEM((2, KV_HEADS, SPAN - 1, T, HEAD), bf16),
            dma((KV_HEADS, 2)),
            dma((KV_HEADS, 2)),
            dma((KV_HEADS, SPAN - 1, 2)),
            dma((KV_HEADS, SPAN - 1, 2)),
            dma((KV_HEADS, SPAN - 1, 2)),
            dma((KV_HEADS, SPAN - 1, 2)),
        ],
        compiler_params=pltpu.CompilerParams(
            collective_id=0, has_side_effects=True, vmem_limit_bytes=48 * 1024 * 1024
        ),
        name="attention",
    )(queries, keys, values, out_grad, doc_lengths)


def solution(mesh):
    rows = P(("blk", "inner"), None)
    return jax.shard_map(
        local,
        mesh=mesh,
        in_specs=(rows, rows, rows, rows, P()),
        out_specs=(rows, rows, rows, rows),
        check_vma=False,
    )
```

profile of v0, /device:TPU:0, one launch (start us, length us, event | category | flops | bytes accessed | tf_op | source)
XLA Modules:
  0.0 80.6 jit_solution(15810748622436720735)
XLA Ops:
  0.6 0.0 copy-start
  0.6 0.9 %copy-done = bf16[256,512]{1,0:T(8,128)(2,1)S(1)} copy-done((bf16[256,512]{1,0:T(8,128)(2,1)S(1)}, bf16[256,512]{1,0:T(8,128)(2,1)}, u32[]{:S(2)}) %copy-start) | copy-done | bytes 262168
  1.6 0.0 copy-start.1
  1.6 0.9 %copy-done.1 = bf16[256,512]{1,0:T(8,128)(2,1)S(1)} copy-done((bf16[256,512]{1,0:T(8,128)(2,1)S(1)}, bf16[256,512]{1,0:T(8,128)(2,1)}, u32[]{:S(2)}) %copy-start.1) | copy-done | bytes 262168
  2.5 0.0 copy-start.2
  2.5 0.7 copy-done.2
  3.2 73.3 %attention.1 = (bf16[256,4096]{1,0:T(8,128)(2,1)S(1)}, bf16[256,4096]{1,0:T(8,128)(2,1)S(1)}, bf16[256,512]{1,0:T(8,128)(2,1)S(1)}, bf16[256,512]{1,0:T(8,128)(2,1)S(1)}) custom-call(bf16[256,4096]{1,0:T(8,128)(2,1)} %q_hbm.1, bf16[256,512]{1,0:T(8,128)(2,1)S(1)} %copy-done, bf16[256,512]{1,0:T(8,128)(2,1)S(1)} %copy-done.1, bf16[256,4096]{1,0:T(8,128)(2,1)} %g_hbm.1, ...), custom_call_target="tpu_custom_call" | custom-call | tf_op jit(solution)/shard_map/attention/pallas_call | solution.py:245
  76.5 1.3 %copy.13 = bf16[256,4096]{1,0:T(8,128)(2,1)} copy(bf16[256,4096]{1,0:T(8,128)(2,1)S(1)} %get-tuple-element.8) | data formatting | bytes 4194304
  77.9 1.3 %copy.14 = bf16[256,4096]{1,0:T(8,128)(2,1)} copy(bf16[256,4096]{1,0:T(8,128)(2,1)S(1)} %get-tuple-element.9) | data formatting | bytes 4194304
  79.2 0.7 copy.15
  79.9 0.7 copy.16
Async XLA Ops:
  0.6 1.0 %copy-start = (bf16[256,512]{1,0:T(8,128)(2,1)S(1)}, bf16[256,512]{1,0:T(8,128)(2,1)}, u32[]{:S(2)}) copy-start(bf16[256,512]{1,0:T(8,128)(2,1)} %k_hbm.1) | copy-start | bytes 786436
  1.6 0.9 %copy-start.1 = (bf16[256,512]{1,0:T(8,128)(2,1)S(1)}, bf16[256,512]{1,0:T(8,128)(2,1)}, u32[]{:S(2)}) copy-start(bf16[256,512]{1,0:T(8,128)(2,1)} %v_hbm.1) | copy-start | bytes 786436
  2.5 0.7 copy-start.2
where the time goes:
time: 80.8 us; the launch traced here: 80.6 us
  Pallas kernels  73.3 us (91%)
  local copies, waits for them, and re-layouts  6.59 us (8%)
    pallas_call x1, Pallas kernels, local(): pl.pallas_call(kernel, out_shape=(jax.ShapeDtypeStruct(queries.shape, bf1...  73.3 us
    unnamed x10, local copies, waits for them, and re-layouts  6.59 us

commit v1 on v0

--- a/solution.py
+++ b/solution.py
@@ -11,6 +11,7 @@
 KV_HEADS = 4
 GROUP = 8
 SPAN = 4
+RING = 4
 SUB = 128
 MESH = pl.DeviceIdType.MESH
 NT = (((1,), (1,)), ((), ()))
@@ -34,7 +35,7 @@
     k_hbm,
     v_hbm,
     g_hbm,
-    len_ref,
+    len_hbm,
     att_ref,
     dq_ref,
     dk_ref,
@@ -52,12 +53,20 @@
     own,
     out_part,
     in_part,
+    relay_out,
+    relay_in,
+    len_ref,
     load_sem,
     own_sem,
-    send_sem,
-    recv_sem,
+    len_sem,
+    cross_send,
+    cross_recv,
+    share_send,
+    share_recv,
     back_send,
     back_recv,
+    relay_send,
+    relay_recv,
 ):
     T = q_hbm.shape[0]
     W = SPAN * T
@@ -72,6 +81,12 @@
         there = lax.rem(me + offset + count, count)
         return (there // inner, lax.rem(there, inner))
 
+    place = lax.rem(me, RING)
+
+    def member(offset):
+        there = me - place + lax.rem(place + offset + RING, RING)
+        return (there // inner, lax.rem(there, inner))
+
     def load(j, which):
         src, dst = ((q_hbm, q_v), (g_hbm, g_v))[which]
         at = pl.ds(pl.multiple_of(j * cols, cols), cols)
@@ -84,46 +99,97 @@
             src.at[:, at], win.at[which, j, pl.ds(W - T, T), :], own_sem.at[j, which]
         )
 
-    def send(j, d, which):
-        src = (k_hbm, v_hbm)[which]
-        at = pl.ds(pl.multiple_of(j * HEAD, HEAD), HEAD)
+    def cross(j, which):
         return pltpu.make_async_remote_copy(
-            src_ref=src.at[:, at],
-            dst_ref=win.at[which, j, pl.ds((SPAN - 1 - d) * T, T), :],
-            send_sem=send_sem.at[j, d - 1, which],
-            recv_sem=recv_sem.at[j, d - 1, which],
-            device_id=device(d),
+            src_ref=win.at[which, j, pl.ds(W - T, T), :],
+            dst_ref=win.at[which, j, pl.ds(W, T), :],
+            send_sem=cross_send.at[j, which],
+            recv_sem=cross_recv.at[j, which],
+            device_id=device(RING),
             device_id_type=MESH,
         )
 
-    def back(j, d, which):
+    def share(j, m, which, relayed):
         return pltpu.make_async_remote_copy(
-            src_ref=out_part.at[which, j, pl.ds((SPAN - 1 - d) * T, T), :],
-            dst_ref=in_part.at[which, j, d - 1],
-            send_sem=back_send.at[j, d - 1, which],
-            recv_sem=back_recv.at[j, d - 1, which],
-            device_id=device(-d),
+            src_ref=win.at[which, j, pl.ds(W if relayed else W - T, T), :],
+            dst_ref=win.at[which, j, pl.ds((SPAN - 1 - m) * T, T), :],
+            send_sem=share_send.at[j, m - 1, which],
+            recv_sem=share_recv.at[j, m - 1, which],
+            device_id=member(m),
             device_id_type=MESH,
         )
 
+    def back(j, m, which):
+        return pltpu.make_async_remote_copy(
+            src_ref=out_part.at[which, j, pl.ds((SPAN - 1 - m) * T, T), :],
+            dst_ref=in_part.at[which, j, m - 1],
+            send_sem=back_send.at[j, m - 1, which],
+            recv_sem=back_recv.at[j, m - 1, which],
+            device_id=member(-m),
+            device_id_type=MESH,
+        )
+
+    def cross_back(j, which):
+        return pltpu.make_async_remote_copy(
+            src_ref=relay_out.at[which, j],
+            dst_ref=relay_in.at[which, j],
+            send_sem=relay_send.at[j, which],
+            recv_sem=relay_recv.at[j, which],
+            device_id=device(-RING),
+            device_id_type=MESH,
+        )
+
     def each(fn):
-        for d in range(1, SPAN):
+        for m in range(1, SPAN):
             for which in range(2):
-                fn(d, which)
+                fn(m, which)
+
+    def start_shares(j):
+        for m in range(1, SPAN):
+
+            @pl.when(place + m < RING)
+            def _():
+                for which in range(2):
+                    share(j, m, which, False).start()
+
+        for which in range(2):
+            cross(j, which).wait_recv()
+        for m in range(1, SPAN):
+
+            @pl.when(place + m >= RING)
+            def _():
+                for which in range(2):
+                    share(j, m, which, True).start()
 
     barrier = pltpu.get_barrier_semaphore()
-    for d in range(1, SPAN):
-        for sign in (1, -1):
-            pl.semaphore_signal(barrier, inc=1, device_id=device(sign * d), device_id_type=MESH)
+    for m in range(1, RING):
+        pl.semaphore_signal(barrier, inc=1, device_id=member(m), device_id_type=MESH)
+    for sign in (1, -1):
+        pl.semaphore_signal(barrier, inc=1, device_id=device(sign * RING), device_id_type=MESH)
 
     @pl.loop(0, KV_HEADS)
     def _(j):
         for which in range(2):
             own_copy(j, which).start()
+
+    lengths = pltpu.make_async_copy(len_hbm, len_ref, len_sem)
+    lengths.start()
+
+    @pl.loop(0, KV_HEADS)
+    def _(j):
+        for which in range(2):
             load(j, which).start()
 
-    pl.semaphore_wait(barrier, 2 * (SPAN - 1))
-    each(lambda d, which: send(0, d, which).start())
+    pl.semaphore_wait(barrier, RING + 1)
+
+    @pl.loop(0, KV_HEADS)
+    def _(j):
+        for which in range(2):
+            own_copy(j, which).wait()
+            cross(j, which).start()
+
+    start_shares(0)
+    lengths.wait()
 
     q_pos = me * T + lax.broadcasted_iota(jnp.int32, (8, T), 1)
 
@@ -144,16 +210,29 @@
             ok = (k_pos >= low) & (k_pos <= high)
             bias[sub, c * SUB : (c + 1) * SUB, :] = jnp.where(ok, 0.0, -1e30)
 
+    def relay(j):
+        each(lambda m, which: back(j, m, which).wait_recv())
+        for which in range(2):
+            mine = own[which, j]
+            theirs = jnp.zeros((T, HEAD), jnp.float32)
+            for m in range(1, SPAN):
+                part = in_part[which, j, m - 1].astype(jnp.float32)
+                keep = place + m < RING
+                mine = mine + jnp.where(keep, part, 0.0)
+                theirs = theirs + jnp.where(keep, 0.0, part)
+            own[which, j] = mine
+            relay_out[which, j] = theirs.astype(jnp.bfloat16)
+            cross_back(j, which).start()
+
     @pl.loop(0, KV_HEADS)
     def _(j):
         @pl.when(j + 1 < KV_HEADS)
         def _():
-            each(lambda d, which: send(j + 1, d, which).start())
-
-        for which in range(2):
-            own_copy(j, which).wait()
+            start_shares(j + 1)
+
+        for which in range(2):
             load(j, which).wait()
-        each(lambda d, which: send(j, d, which).wait_recv())
+        each(lambda m, which: share(j, m, which, False).wait_recv())
         for which in range(2):
             for r in range(0, W, SUB):
                 win_t[which, :, r : r + SUB] = win[which, j, r : r + SUB, :].T
@@ -216,22 +295,29 @@
             factor = scale if which == 0 else 1.0
             out_part[which, j] = (acc[which, : W - T, :] * factor).astype(jnp.bfloat16)
             own[which, j] = acc[which, W - T :, :] * factor
-        each(lambda d, which: back(j, d, which).start())
-
-    @pl.loop(0, KV_HEADS)
-    def _(j):
-        each(lambda d, which: back(j, d, which).wait_recv())
+        each(lambda m, which: back(j, m, which).start())
+
+        @pl.when(j > 0)
+        def _():
+            relay(j - 1)
+
+    relay(KV_HEADS - 1)
+
+    @pl.loop(0, KV_HEADS)
+    def _(j):
         at = pl.ds(pl.multiple_of(j * HEAD, HEAD), HEAD)
         for which, ref in ((0, dk_ref), (1, dv_ref)):
-            sums = own[which, j]
-            for d in range(1, SPAN):
-                sums = sums + in_part[which, j, d - 1].astype(jnp.float32)
+            cross_back(j, which).wait_recv()
+            sums = own[which, j] + relay_in[which, j].astype(jnp.float32)
             ref[:, at] = sums.astype(jnp.bfloat16)
 
     @pl.loop(0, KV_HEADS)
     def _(j):
-        each(lambda d, which: send(j, d, which).wait_send())
-        each(lambda d, which: back(j, d, which).wait_send())
+        each(lambda m, which: share(j, m, which, False).wait_send())
+        each(lambda m, which: back(j, m, which).wait_send())
+        for which in range(2):
+            cross(j, which).wait_send()
+            cross_back(j, which).wait_send()
 
 
 def local(queries, keys, values, out_grad, doc_lengths):
@@ -239,7 +325,7 @@
     W = SPAN * T
     WIN = W - SUB
     bf16, f32 = jnp.bfloat16, jnp.float32
-    anywhere = pl.BlockSpec(memory_space=pl.ANY)
+    hbm = pl.BlockSpec(memory_space=pltpu.HBM)
     vmem = pl.BlockSpec(memory_space=pltpu.VMEM)
     dma = pltpu.SemaphoreType.DMA
     return pl.pallas_call(
@@ -250,12 +336,12 @@
             jax.ShapeDtypeStruct(keys.shape, bf16),
             jax.ShapeDtypeStruct(keys.shape, bf16),
         ),
-        in_specs=[anywhere] * 4 + [pl.BlockSpec(memory_space=pltpu.SMEM)],
+        in_specs=[hbm] * 5,
         out_specs=(vmem, vmem, vmem, vmem),
         scratch_shapes=[
             pltpu.VMEM((KV_HEADS, T, GROUP * HEAD), bf16),
             pltpu.VMEM((KV_HEADS, T, GROUP * HEAD), bf16),
-            pltpu.VMEM((2, KV_HEADS, W, HEAD), bf16),
+            pltpu.VMEM((2, KV_HEADS, W + T, HEAD), bf16),
             pltpu.VMEM((2, HEAD, W), bf16),
             pltpu.VMEM((T // SUB, WIN, SUB), f32),
             pltpu.VMEM((WIN, 2 * SUB), f32),
@@ -266,12 +352,20 @@
             pltpu.VMEM((2, KV_HEADS, T, HEAD), f32),
             pltpu.VMEM((2, KV_HEADS, W - T, HEAD), bf16),
             pltpu.VMEM((2, KV_HEADS, SPAN - 1, T, HEAD), bf16),
+            pltpu.VMEM((2, KV_HEADS, T, HEAD), bf16),
+            pltpu.VMEM((2, KV_HEADS, T, HEAD), bf16),
+            pltpu.SMEM(doc_lengths.shape, jnp.int32),
+            dma((KV_HEADS, 2)),
+            dma((KV_HEADS, 2)),
+            dma(()),
             dma((KV_HEADS, 2)),
             dma((KV_HEADS, 2)),
             dma((KV_HEADS, SPAN - 1, 2)),
             dma((KV_HEADS, SPAN - 1, 2)),
             dma((KV_HEADS, SPAN - 1, 2)),
             dma((KV_HEADS, SPAN - 1, 2)),
+            dma((KV_HEADS, 2)),
+            dma((KV_HEADS, 2)),
         ],
         compiler_params=pltpu.CompilerParams(
             collective_id=0, has_side_effects=True, vmem_limit_bytes=48 * 1024 * 1024

time: 80.8 us -> 85.8 us (1.062)
  Pallas kernels: 73.3 us -> 78.4 us
    pallas_call x1, Pallas kernels: 73.3 us -> 78.4 us  [local(): pl.pallas_call(kernel, out_shape=(jax.ShapeDtypeStruct(queries.shape, bf1...]
where the time goes in v1:
time: 85.8 us; the launch traced here: 85.6 us
  Pallas kernels  78.4 us (91%)
  local copies, waits for them, and re-layouts  6.59 us (8%)
    pallas_call x1, Pallas kernels, local(): pl.pallas_call(kernel, out_shape=(jax.ShapeDtypeStruct(queries.shape, bf1...  78.4 us
    unnamed x10, local copies, waits for them, and re-layouts  6.59 us

profile of v1, /device:TPU:0, one launch (start us, length us, event | category | flops | bytes accessed | tf_op | source)
XLA Modules:
  0.0 85.6 jit_solution(3664450240130125594)
XLA Ops:
  0.6 0.0 copy-start
  0.6 0.9 %copy-done = bf16[256,512]{1,0:T(8,128)(2,1)S(1)} copy-done((bf16[256,512]{1,0:T(8,128)(2,1)S(1)}, bf16[256,512]{1,0:T(8,128)(2,1)}, u32[]{:S(2)}) %copy-start) | copy-done | bytes 262168
  1.6 0.0 copy-start.1
  1.6 0.9 %copy-done.1 = bf16[256,512]{1,0:T(8,128)(2,1)S(1)} copy-done((bf16[256,512]{1,0:T(8,128)(2,1)S(1)}, bf16[256,512]{1,0:T(8,128)(2,1)}, u32[]{:S(2)}) %copy-start.1) | copy-done | bytes 262168
  2.5 0.0 copy-start.2
  2.5 0.7 copy-done.2
  3.2 78.4 %attention.1 = (bf16[256,4096]{1,0:T(8,128)(2,1)S(1)}, bf16[256,4096]{1,0:T(8,128)(2,1)S(1)}, bf16[256,512]{1,0:T(8,128)(2,1)S(1)}, bf16[256,512]{1,0:T(8,128)(2,1)S(1)}) custom-call(bf16[256,4096]{1,0:T(8,128)(2,1)} %q_hbm.1, bf16[256,512]{1,0:T(8,128)(2,1)S(1)} %copy-done, bf16[256,512]{1,0:T(8,128)(2,1)S(1)} %copy-done.1, bf16[256,4096]{1,0:T(8,128)(2,1)} %g_hbm.1, ...), custom_call_target="tpu_custom_call" | custom-call | tf_op jit(solution)/shard_map/attention/pallas_call | solution.py:331
  81.6 1.3 %copy.13 = bf16[256,4096]{1,0:T(8,128)(2,1)} copy(bf16[256,4096]{1,0:T(8,128)(2,1)S(1)} %get-tuple-element.8) | data formatting | bytes 4194304
  82.9 1.3 %copy.14 = bf16[256,4096]{1,0:T(8,128)(2,1)} copy(bf16[256,4096]{1,0:T(8,128)(2,1)S(1)} %get-tuple-element.9) | data formatting | bytes 4194304
  84.2 0.7 copy.15
  84.9 0.7 copy.16
Async XLA Ops:
  0.6 1.0 %copy-start = (bf16[256,512]{1,0:T(8,128)(2,1)S(1)}, bf16[256,512]{1,0:T(8,128)(2,1)}, u32[]{:S(2)}) copy-start(bf16[256,512]{1,0:T(8,128)(2,1)} %k_hbm.1) | copy-start | bytes 786436
  1.6 0.9 %copy-start.1 = (bf16[256,512]{1,0:T(8,128)(2,1)S(1)}, bf16[256,512]{1,0:T(8,128)(2,1)}, u32[]{:S(2)}) copy-start(bf16[256,512]{1,0:T(8,128)(2,1)} %v_hbm.1) | copy-start | bytes 786436
  2.5 0.7 copy-start.2

commit v2 on v0

--- a/solution.py
+++ b/solution.py
@@ -34,7 +34,7 @@
     k_hbm,
     v_hbm,
     g_hbm,
-    len_ref,
+    len_hbm,
     att_ref,
     dq_ref,
     dk_ref,
@@ -52,6 +52,8 @@
     own,
     out_part,
     in_part,
+    len_ref,
+    len_sem,
     load_sem,
     own_sem,
     send_sem,
@@ -116,6 +118,9 @@
         for sign in (1, -1):
             pl.semaphore_signal(barrier, inc=1, device_id=device(sign * d), device_id_type=MESH)
 
+    lengths = pltpu.make_async_copy(len_hbm, len_ref, len_sem)
+    lengths.start()
+
     @pl.loop(0, KV_HEADS)
     def _(j):
         for which in range(2):
@@ -124,6 +129,8 @@
 
     pl.semaphore_wait(barrier, 2 * (SPAN - 1))
     each(lambda d, which: send(0, d, which).start())
+
+    lengths.wait()
 
     q_pos = me * T + lax.broadcasted_iota(jnp.int32, (8, T), 1)
 
@@ -234,6 +241,15 @@
         each(lambda d, which: back(j, d, which).wait_send())
 
 
+def place_results(*refs):
+    sem = refs[-1]
+    copies = [pltpu.make_async_copy(refs[i], refs[4 + i], sem.at[i]) for i in range(4)]
+    for copy in copies:
+        copy.start()
+    for copy in copies:
+        copy.wait()
+
+
 def local(queries, keys, values, out_grad, doc_lengths):
     T = queries.shape[0]
     W = SPAN * T
@@ -242,7 +258,7 @@
     anywhere = pl.BlockSpec(memory_space=pl.ANY)
     vmem = pl.BlockSpec(memory_space=pltpu.VMEM)
     dma = pltpu.SemaphoreType.DMA
-    return pl.pallas_call(
+    parts = pl.pallas_call(
         kernel,
         out_shape=(
             jax.ShapeDtypeStruct(queries.shape, bf16),
@@ -250,7 +266,7 @@
             jax.ShapeDtypeStruct(keys.shape, bf16),
             jax.ShapeDtypeStruct(keys.shape, bf16),
         ),
-        in_specs=[anywhere] * 4 + [pl.BlockSpec(memory_space=pltpu.SMEM)],
+        in_specs=[anywhere] * 5,
         out_specs=(vmem, vmem, vmem, vmem),
         scratch_shapes=[
             pltpu.VMEM((KV_HEADS, T, GROUP * HEAD), bf16),
@@ -266,6 +282,8 @@
             pltpu.VMEM((2, KV_HEADS, T, HEAD), f32),
             pltpu.VMEM((2, KV_HEADS, W - T, HEAD), bf16),
             pltpu.VMEM((2, KV_HEADS, SPAN - 1, T, HEAD), bf16),
+            pltpu.SMEM(doc_lengths.shape, jnp.int32),
+            dma(()),
             dma((KV_HEADS, 2)),
             dma((KV_HEADS, 2)),
             dma((KV_HEADS, SPAN - 1, 2)),
@@ -277,7 +295,21 @@
             collective_id=0, has_side_effects=True, vmem_limit_bytes=48 * 1024 * 1024
         ),
         name="attention",
-    )(queries, keys, values, out_grad, doc_lengths)
+    )(
+        *(
+            pltpu.with_memory_space_constraint(x, pltpu.HBM)
+            for x in (queries, keys, values, out_grad, doc_lengths)
+        )
+    )
+    return pl.pallas_call(
+        place_results,
+        out_shape=tuple(jax.ShapeDtypeStruct(x.shape, x.dtype) for x in parts),
+        in_specs=[vmem] * 4,
+        out_specs=(anywhere,) * 4,
+        scratch_shapes=[dma((4,))],
+        compiler_params=pltpu.CompilerParams(vmem_limit_bytes=1024 * 1024),
+        name="results",
+    )(*(pltpu.with_memory_space_constraint(x, pltpu.VMEM) for x in parts))
 
 
 def solution(mesh):

time: 80.8 us -> 76 us (0.941)
  local copies, waits for them, and re-layouts: 6.59 us -> 0 us
  Pallas kernels: 73.3 us -> 75.3 us
    unnamed x10 -> x0, local copies, waits for them, and re-layouts: 6.59 us -> none
    pallas_call x0 -> x1, Pallas kernels: none -> 2.2 us  [local(): pl.pallas_call(place_results, out_shape=tuple((jax.ShapeDtypeStruct(x.sha...]
where the time goes in v2:
time: 76 us; the launch traced here: 75.9 us
  Pallas kernels  75.3 us (99%)
    pallas_call x1, Pallas kernels, local(): pl.pallas_call(kernel, out_shape=(jax.ShapeDtypeStruct(queries.shape, bf1...  73.1 us
    pallas_call x1, Pallas kernels, local(): pl.pallas_call(place_results, out_shape=tuple((jax.ShapeDtypeStruct(x.sha...  2.2 us

profile of v2, /device:TPU:0, one launch (start us, length us, event | category | flops | bytes accessed | tf_op | source)
XLA Modules:
  0.0 75.9 jit_solution(6305132646078021380)
XLA Ops:
  0.6 73.1 %attention.1 = (bf16[256,4096]{1,0:T(8,128)(2,1)S(1)}, bf16[256,4096]{1,0:T(8,128)(2,1)S(1)}, bf16[256,512]{1,0:T(8,128)(2,1)S(1)}, bf16[256,512]{1,0:T(8,128)(2,1)S(1)}) custom-call(bf16[256,4096]{1,0:T(8,128)(2,1)} %q_hbm.1, bf16[256,512]{1,0:T(8,128)(2,1)} %k_hbm.1, bf16[256,512]{1,0:T(8,128)(2,1)} %v_hbm.1, bf16[256,4096]{1,0:T(8,128)(2,1)} %g_hbm.1, ...), custom_call_target="tpu_custom_call" | custom-call | tf_op jit(solution)/shard_map/attention/pallas_call | solution.py:261
  73.7 2.2 %results.1 = (bf16[256,4096]{1,0:T(8,128)(2,1)}, bf16[256,4096]{1,0:T(8,128)(2,1)}, bf16[256,512]{1,0:T(8,128)(2,1)}, bf16[256,512]{1,0:T(8,128)(2,1)}) custom-call(bf16[256,4096]{1,0:T(8,128)(2,1)S(1)} %get-tuple-element.8.refs_0_, bf16[256,4096]{1,0:T(8,128)(2,1)S(1)} %get-tuple-element.9.refs_1_, bf16[256,512]{1,0:T(8,128)(2,1)S(1)} %get-tuple-element.10.refs_2_, ...), custom_call_target="tpu_custom_call" | custom-call | tf_op jit(solution)/shard_map/results/pallas_call | solution.py:304

commit v3 on v2

--- a/solution.py
+++ b/solution.py
@@ -12,6 +12,9 @@
 GROUP = 8
 SPAN = 4
 SUB = 128
+PATTERN = "bbabbabbababaaba"
+AH = 4
+BH = 7
 MESH = pl.DeviceIdType.MESH
 NT = (((1,), (1,)), ((), ()))
 NN = (((1,), (0,)), ((), ()))
@@ -44,8 +47,9 @@
     win,
     win_t,
     bias,
-    s_ref,
+    p_ref,
     dp_ref,
+    stats,
     w_ref,
     ds_ref,
     acc,
@@ -131,7 +135,6 @@
     each(lambda d, which: send(0, d, which).start())
 
     lengths.wait()
-
     q_pos = me * T + lax.broadcasted_iota(jnp.int32, (8, T), 1)
 
     def doc_step(i, carry):
@@ -151,73 +154,123 @@
             ok = (k_pos >= low) & (k_pos <= high)
             bias[sub, c * SUB : (c + 1) * SUB, :] = jnp.where(ok, 0.0, -1e30)
 
+    chunks = WIN // SUB
+    to_exp2 = scale * math.log2(math.e)
+
+    def arrive(j):
+        each(lambda d, which: send(j, d, which).wait_recv())
+
+    def stacked(ref, j, pair, sub):
+        rows = slice(sub * SUB, (sub + 1) * SUB)
+        parts = [
+            ref[j, rows, pl.ds(pl.multiple_of((pair * 2 + side) * HEAD, HEAD), HEAD)]
+            for side in range(2)
+        ]
+        return jnp.concatenate(parts, axis=0)
+
+    def ahead(j, pair, sub):
+        qu, gu = stacked(q_v, j, pair, sub), stacked(g_v, j, pair, sub)
+        for c in range(chunks):
+            at = slice(c * SUB, (c + 1) * SUB)
+            keys = slice((sub + c) * SUB, (sub + c + 1) * SUB)
+            extra = bias[sub, at, :]
+            if c % AH == 0:
+                wide = slice((sub + c) * SUB, (sub + min(c + AH, chunks)) * SUB)
+                s_wide = dot(win[0, j, wide, :], qu, NT)
+                dp_wide = dot(win[1, j, wide, :], gu, NT)
+            part = slice(c % AH * SUB, (c % AH + 1) * SUB)
+            s = s_wide[part] + jnp.concatenate([extra, extra], axis=1)
+            dp = dp_wide[part]
+            top = jnp.max(fold_rows(s, jnp.maximum), axis=0, keepdims=True)
+            p = jnp.exp2((s - top) * to_exp2)
+            p_ref[sub, at, :] = p
+            dp_ref[sub, at, :] = dp
+            stats[sub, 0, c] = jnp.broadcast_to(top, (8, 2 * SUB))
+            stats[sub, 1, c] = fold_rows(p, jnp.add)
+            stats[sub, 2, c] = fold_rows(p * dp, jnp.add)
+            yield
+
+    def behind(j, pair, sub):
+        qu, gu = stacked(q_v, j, pair, sub), stacked(g_v, j, pair, sub)
+        rows = slice(sub * SUB, (sub + 1) * SUB)
+        tops = [stats[sub, 0, c] for c in range(chunks)]
+        top = tops[0]
+        for c in range(1, chunks):
+            top = jnp.maximum(top, tops[c])
+        factors = [jnp.exp2((tops[c] - top) * to_exp2) for c in range(chunks)]
+        total = sum(stats[sub, 1, c] * factors[c] for c in range(chunks))
+        cross = sum(stats[sub, 2, c] * factors[c] for c in range(chunks))
+        inv = 1.0 / jnp.sum(total, axis=0, keepdims=True)
+        delta = jnp.sum(cross, axis=0, keepdims=True) * inv
+        for c in range(chunks):
+            at = slice(c * SUB, (c + 1) * SUB)
+            keys = slice((sub + c) * SUB, (sub + c + 1) * SUB)
+            w = p_ref[sub, at, :] * (factors[c][0:1] * inv)
+            ds = (w * (dp_ref[sub, at, :] - delta)).astype(jnp.bfloat16)
+            w = w.astype(jnp.bfloat16)
+            w_ref[sub, at, :] = w
+            ds_ref[sub, at, :] = ds
+            if (c + 1) % BH == 0 or c + 1 == chunks:
+                low = c // BH * BH
+                wide = slice((sub + low) * SUB, (sub + c + 1) * SUB)
+                acc[0, wide, :] += dot(ds_ref[sub, low * SUB : (c + 1) * SUB, :], qu, NN)
+                acc[1, wide, :] += dot(w_ref[sub, low * SUB : (c + 1) * SUB, :], gu, NN)
+            yield
+        span = slice(sub * SUB, sub * SUB + WIN)
+        for out, left, right, factor in (
+            (att_ref, 1, w_ref, 1.0),
+            (dq_ref, 0, ds_ref, scale),
+        ):
+            product = dot(win_t[left, :, span], right[sub], NN)
+            for side in range(2):
+                at = pl.ds(pl.multiple_of(j * cols + (pair * 2 + side) * HEAD, HEAD), HEAD)
+                tile = product[:, side * SUB : (side + 1) * SUB]
+                out[rows, at] = (tile.T * factor).astype(jnp.bfloat16)
+            yield
+
+    def together(first, second, pattern):
+        for letter in pattern:
+            next(first if letter == "b" else second, None)
+
+    pairs = GROUP // 2
+
+    @pl.loop(0, KV_HEADS)
+    def _(j):
+        for which in range(2):
+            own_copy(j, which).wait()
+            load(j, which).wait()
+
+    arrive(0)
+    for _ in ahead(0, 0, 0):
+        pass
+
     @pl.loop(0, KV_HEADS)
     def _(j):
         @pl.when(j + 1 < KV_HEADS)
         def _():
             each(lambda d, which: send(j + 1, d, which).start())
 
-        for which in range(2):
-            own_copy(j, which).wait()
-            load(j, which).wait()
-        each(lambda d, which: send(j, d, which).wait_recv())
         for which in range(2):
             for r in range(0, W, SUB):
                 win_t[which, :, r : r + SUB] = win[which, j, r : r + SUB, :].T
         acc[...] = jnp.zeros_like(acc)
 
-        def unit(pair, sub):
-            rows = slice(sub * SUB, (sub + 1) * SUB)
-            col0 = pl.ds(pl.multiple_of(pair * 2 * HEAD, HEAD), HEAD)
-            col1 = pl.ds(pl.multiple_of(pair * 2 * HEAD + HEAD, HEAD), HEAD)
-            out0 = pl.ds(pl.multiple_of(j * cols + pair * 2 * HEAD, HEAD), HEAD)
-            out1 = pl.ds(pl.multiple_of(j * cols + pair * 2 * HEAD + HEAD, HEAD), HEAD)
-            qu = jnp.concatenate([q_v[j, rows, col0], q_v[j, rows, col1]], axis=0)
-            gu = jnp.concatenate([g_v[j, rows, col0], g_v[j, rows, col1]], axis=0)
-
-            def keys(c):
-                return slice((sub + c) * SUB, (sub + c + 1) * SUB)
-
-            top = None
-            for c in range(WIN // SUB):
-                at = slice(c * SUB, (c + 1) * SUB)
-                extra = bias[sub, at, :]
-                s = dot(win[0, j, keys(c), :], qu, NT) + jnp.concatenate([extra, extra], axis=1)
-                s_ref[at, :] = s
-                part = fold_rows(s, jnp.maximum)
-                top = part if top is None else jnp.maximum(top, part)
-            top = jnp.max(top, axis=0, keepdims=True)
-            total = jnp.zeros((8, 2 * SUB), jnp.float32)
-            cross = jnp.zeros((8, 2 * SUB), jnp.float32)
-            for c in range(WIN // SUB):
-                at = slice(c * SUB, (c + 1) * SUB)
-                p = jnp.exp2((s_ref[at, :] - top) * (scale * math.log2(math.e)))
-                dp = dot(win[1, j, keys(c), :], gu, NT)
-                total = total + fold_rows(p, jnp.add)
-                cross = cross + fold_rows(p * dp, jnp.add)
-                s_ref[at, :] = p
-                dp_ref[at, :] = dp
-            inv = 1.0 / jnp.sum(total, axis=0, keepdims=True)
-            delta = jnp.sum(cross, axis=0, keepdims=True) * inv
-            for c in range(WIN // SUB):
-                at = slice(c * SUB, (c + 1) * SUB)
-                w = s_ref[at, :] * inv
-                w_ref[at, :] = w.astype(jnp.bfloat16)
-                ds_ref[at, :] = (w * (dp_ref[at, :] - delta)).astype(jnp.bfloat16)
-            span = slice(sub * SUB, sub * SUB + WIN)
-            o_t = dot(win_t[1, :, span], w_ref[...], NN)
-            dq_t = dot(win_t[0, :, span], ds_ref[...], NN) * scale
-            att_ref[rows, out0] = o_t[:, :SUB].T.astype(jnp.bfloat16)
-            att_ref[rows, out1] = o_t[:, SUB:].T.astype(jnp.bfloat16)
-            dq_ref[rows, out0] = dq_t[:, :SUB].T.astype(jnp.bfloat16)
-            dq_ref[rows, out1] = dq_t[:, SUB:].T.astype(jnp.bfloat16)
-            acc[0, span, :] += dot(ds_ref[...], qu, NN)
-            acc[1, span, :] += dot(w_ref[...], gu, NN)
-
-        @pl.loop(0, GROUP // 2)
+        @pl.loop(0, pairs - 1)
         def _(pair):
-            for sub in range(T // SUB):
-                unit(pair, sub)
+            together(behind(j, pair, 0), ahead(j, pair, 1), PATTERN)
+            together(behind(j, pair, 1), ahead(j, pair + 1, 0), PATTERN)
+
+        together(behind(j, pairs - 1, 0), ahead(j, pairs - 1, 1), PATTERN)
+
+        @pl.when(j + 1 < KV_HEADS)
+        def _():
+            arrive(j + 1)
+            together(behind(j, pairs - 1, 1), ahead(j + 1, 0, 0), PATTERN)
+
+        @pl.when(j + 1 == KV_HEADS)
+        def _():
+            for _ in behind(j, pairs - 1, 1):
+                pass
 
         for which in range(2):
             factor = scale if which == 0 else 1.0
@@ -274,10 +327,11 @@
             pltpu.VMEM((2, KV_HEADS, W, HEAD), bf16),
             pltpu.VMEM((2, HEAD, W), bf16),
             pltpu.VMEM((T // SUB, WIN, SUB), f32),
-            pltpu.VMEM((WIN, 2 * SUB), f32),
-            pltpu.VMEM((WIN, 2 * SUB), f32),
-            pltpu.VMEM((WIN, 2 * SUB), bf16),
-            pltpu.VMEM((WIN, 2 * SUB), bf16),
+            pltpu.VMEM((2, WIN, 2 * SUB), f32),
+            pltpu.VMEM((2, WIN, 2 * SUB), f32),
+            pltpu.VMEM((2, 3, WIN // SUB, 8, 2 * SUB), f32),
+            pltpu.VMEM((2, WIN, 2 * SUB), bf16),
+            pltpu.VMEM((2, WIN, 2 * SUB), bf16),
             pltpu.VMEM((2, W, HEAD), f32),
             pltpu.VMEM((2, KV_HEADS, T, HEAD), f32),
             pltpu.VMEM((2, KV_HEADS, W - T, HEAD), bf16),

time: 76 us -> 76.7 us (level); the launches traced: 75.9 us -> 75.2 us
  no operation moved by 1% of the time
where the time goes in v3:
time: 76.7 us; the launch traced here: 75.2 us
  Pallas kernels  74.6 us (97%)
    pallas_call x1, Pallas kernels, local(): pl.pallas_call(kernel, out_shape=(jax.ShapeDtypeStruct(queries.shape, bf1...  72.4 us
    pallas_call x1, Pallas kernels, local(): pl.pallas_call(place_results, out_shape=tuple((jax.ShapeDtypeStruct(x.sha...  2.2 us

profile of v3, /device:TPU:0, one launch (start us, length us, event | category | flops | bytes accessed | tf_op | source)
XLA Modules:
  0.0 75.2 jit_solution(13182605394147788020)
XLA Ops:
  0.6 72.4 %attention.1 = (bf16[256,4096]{1,0:T(8,128)(2,1)S(1)}, bf16[256,4096]{1,0:T(8,128)(2,1)S(1)}, bf16[256,512]{1,0:T(8,128)(2,1)S(1)}, bf16[256,512]{1,0:T(8,128)(2,1)S(1)}) custom-call(bf16[256,4096]{1,0:T(8,128)(2,1)} %q_hbm.1, bf16[256,512]{1,0:T(8,128)(2,1)} %k_hbm.1, bf16[256,512]{1,0:T(8,128)(2,1)} %v_hbm.1, bf16[256,4096]{1,0:T(8,128)(2,1)} %g_hbm.1, ...), custom_call_target="tpu_custom_call" | custom-call | tf_op jit(solution)/shard_map/attention/pallas_call | solution.py:314
  73.0 2.2 %results.1 = (bf16[256,4096]{1,0:T(8,128)(2,1)}, bf16[256,4096]{1,0:T(8,128)(2,1)}, bf16[256,512]{1,0:T(8,128)(2,1)}, bf16[256,512]{1,0:T(8,128)(2,1)}) custom-call(bf16[256,4096]{1,0:T(8,128)(2,1)S(1)} %get-tuple-element.8.refs_0_, bf16[256,4096]{1,0:T(8,128)(2,1)S(1)} %get-tuple-element.9.refs_1_, bf16[256,512]{1,0:T(8,128)(2,1)S(1)} %get-tuple-element.10.refs_2_, ...), custom_call_target="tpu_custom_call" | custom-call | tf_op jit(solution)/shard_map/results/pallas_call | solution.py:358

commit v4 on v3

--- a/solution.py
+++ b/solution.py
@@ -11,6 +11,7 @@
 KV_HEADS = 4
 GROUP = 8
 SPAN = 4
+RING = 4
 SUB = 128
 PATTERN = "bbabbabbababaaba"
 AH = 4
@@ -44,6 +45,7 @@
     dv_ref,
     q_v,
     g_v,
+    own_kv,
     win,
     win_t,
     bias,
@@ -56,14 +58,20 @@
     own,
     out_part,
     in_part,
+    relay_out,
+    relay_in,
     len_ref,
-    len_sem,
     load_sem,
     own_sem,
-    send_sem,
-    recv_sem,
+    len_sem,
+    cross_send,
+    cross_recv,
+    share_send,
+    share_recv,
     back_send,
     back_recv,
+    relay_send,
+    relay_recv,
 ):
     T = q_hbm.shape[0]
     W = SPAN * T
@@ -78,49 +86,94 @@
         there = lax.rem(me + offset + count, count)
         return (there // inner, lax.rem(there, inner))
 
+    place = lax.rem(me, RING)
+
+    def member(offset):
+        there = me - place + lax.rem(place + offset + RING, RING)
+        return (there // inner, lax.rem(there, inner))
+
     def load(j, which):
         src, dst = ((q_hbm, q_v), (g_hbm, g_v))[which]
         at = pl.ds(pl.multiple_of(j * cols, cols), cols)
         return pltpu.make_async_copy(src.at[:, at], dst.at[j], load_sem.at[j, which])
 
-    def own_copy(j, which):
-        src = (k_hbm, v_hbm)[which]
-        at = pl.ds(pl.multiple_of(j * HEAD, HEAD), HEAD)
-        return pltpu.make_async_copy(
-            src.at[:, at], win.at[which, j, pl.ds(W - T, T), :], own_sem.at[j, which]
-        )
-
-    def send(j, d, which):
-        src = (k_hbm, v_hbm)[which]
-        at = pl.ds(pl.multiple_of(j * HEAD, HEAD), HEAD)
+    def own_copy(which):
+        return pltpu.make_async_copy((k_hbm, v_hbm)[which], own_kv.at[which], own_sem.at[which])
+
+    def cross(j):
         return pltpu.make_async_remote_copy(
-            src_ref=src.at[:, at],
-            dst_ref=win.at[which, j, pl.ds((SPAN - 1 - d) * T, T), :],
-            send_sem=send_sem.at[j, d - 1, which],
-            recv_sem=recv_sem.at[j, d - 1, which],
-            device_id=device(d),
+            src_ref=win.at[j, pl.ds(W - T, T), :],
+            dst_ref=win.at[j, pl.ds(W, T), :],
+            send_sem=cross_send.at[j],
+            recv_sem=cross_recv.at[j],
+            device_id=device(RING),
             device_id_type=MESH,
         )
 
-    def back(j, d, which):
+    def share(j, m, relayed):
         return pltpu.make_async_remote_copy(
-            src_ref=out_part.at[which, j, pl.ds((SPAN - 1 - d) * T, T), :],
-            dst_ref=in_part.at[which, j, d - 1],
-            send_sem=back_send.at[j, d - 1, which],
-            recv_sem=back_recv.at[j, d - 1, which],
-            device_id=device(-d),
+            src_ref=win.at[j, pl.ds(W if relayed else W - T, T), :],
+            dst_ref=win.at[j, pl.ds((SPAN - 1 - m) * T, T), :],
+            send_sem=share_send.at[j, m - 1],
+            recv_sem=share_recv.at[j, m - 1],
+            device_id=member(m),
             device_id_type=MESH,
         )
 
+    def back(j, m, which):
+        return pltpu.make_async_remote_copy(
+            src_ref=out_part.at[which, j, pl.ds((SPAN - 1 - m) * T, T), :],
+            dst_ref=in_part.at[which, j, m - 1],
+            send_sem=back_send.at[j, m - 1, which],
+            recv_sem=back_recv.at[j, m - 1, which],
+            device_id=member(-m),
+            device_id_type=MESH,
+        )
+
+    def cross_back(j, which):
+        return pltpu.make_async_remote_copy(
+            src_ref=relay_out.at[which, j],
+            dst_ref=relay_in.at[which, j],
+            send_sem=relay_send.at[j, which],
+            recv_sem=relay_recv.at[j, which],
+            device_id=device(-RING),
+            device_id_type=MESH,
+        )
+
     def each(fn):
-        for d in range(1, SPAN):
-            for which in range(2):
-                fn(d, which)
+        for m in range(1, SPAN):
+            fn(m)
+
+    def start_cross(j):
+        cross(j).start()
+
+    def start_shares(j):
+        start_own(j)
+        start_relayed(j)
+
+    def start_own(j):
+        for m in range(1, SPAN):
+
+            @pl.when(place + m < RING)
+            def _():
+                share(j, m, False).start()
+
+    def start_relayed(j):
+        cross(j).wait_recv()
+        for m in range(1, SPAN):
+
+            @pl.when(place + m >= RING)
+            def _():
+                share(j, m, True).start()
 
     barrier = pltpu.get_barrier_semaphore()
-    for d in range(1, SPAN):
-        for sign in (1, -1):
-            pl.semaphore_signal(barrier, inc=1, device_id=device(sign * d), device_id_type=MESH)
+    for m in range(1, RING):
+        pl.semaphore_signal(barrier, inc=1, device_id=member(m), device_id_type=MESH)
+    for sign in (1, -1):
+        pl.semaphore_signal(barrier, inc=1, device_id=device(sign * RING), device_id_type=MESH)
+
+    for which in range(2):
+        own_copy(which).start()
 
     lengths = pltpu.make_async_copy(len_hbm, len_ref, len_sem)
     lengths.start()
@@ -128,13 +181,21 @@
     @pl.loop(0, KV_HEADS)
     def _(j):
         for which in range(2):
-            own_copy(j, which).start()
             load(j, which).start()
 
-    pl.semaphore_wait(barrier, 2 * (SPAN - 1))
-    each(lambda d, which: send(0, d, which).start())
+    for which in range(2):
+        own_copy(which).wait()
+        for j in range(KV_HEADS):
+            win[j, W - T : W, which * HEAD : (which + 1) * HEAD] = own_kv[
+                which, :, j * HEAD : (j + 1) * HEAD
+            ]
+    pl.semaphore_wait(barrier, RING + 1)
+
+    start_cross(0)
+    start_own(0)
 
     lengths.wait()
+
     q_pos = me * T + lax.broadcasted_iota(jnp.int32, (8, T), 1)
 
     def doc_step(i, carry):
@@ -154,11 +215,34 @@
             ok = (k_pos >= low) & (k_pos <= high)
             bias[sub, c * SUB : (c + 1) * SUB, :] = jnp.where(ok, 0.0, -1e30)
 
+    def relay(j):
+        for which in range(2):
+            each(lambda m: back(j, m, which).wait_recv())
+            mine = own[which, j]
+            theirs = jnp.zeros((T, HEAD), jnp.float32)
+            for m in range(1, SPAN):
+                part = in_part[which, j, m - 1].astype(jnp.float32)
+                keep = place + m < RING
+                mine = mine + jnp.where(keep, part, 0.0)
+                theirs = theirs + jnp.where(keep, 0.0, part)
+            relay_out[which, j] = theirs.astype(jnp.bfloat16)
+            cross_back(j, which).start()
+            own[which, j] = mine
+
+    def finish(j):
+        at = pl.ds(pl.multiple_of(j * HEAD, HEAD), HEAD)
+        for which, ref in ((0, dk_ref), (1, dv_ref)):
+            cross_back(j, which).wait_recv()
+            sums = own[which, j] + relay_in[which, j].astype(jnp.float32)
+            ref[:, at] = sums.astype(jnp.bfloat16)
+
+    start_relayed(0)
+    start_cross(1)
     chunks = WIN // SUB
     to_exp2 = scale * math.log2(math.e)
 
     def arrive(j):
-        each(lambda d, which: send(j, d, which).wait_recv())
+        each(lambda m: share(j, m, False).wait_recv())
 
     def stacked(ref, j, pair, sub):
         rows = slice(sub * SUB, (sub + 1) * SUB)
@@ -176,8 +260,8 @@
             extra = bias[sub, at, :]
             if c % AH == 0:
                 wide = slice((sub + c) * SUB, (sub + min(c + AH, chunks)) * SUB)
-                s_wide = dot(win[0, j, wide, :], qu, NT)
-                dp_wide = dot(win[1, j, wide, :], gu, NT)
+                s_wide = dot(win[j, wide, :HEAD], qu, NT)
+                dp_wide = dot(win[j, wide, HEAD:], gu, NT)
             part = slice(c % AH * SUB, (c % AH + 1) * SUB)
             s = s_wide[part] + jnp.concatenate([extra, extra], axis=1)
             dp = dp_wide[part]
@@ -190,7 +274,7 @@
             stats[sub, 2, c] = fold_rows(p * dp, jnp.add)
             yield
 
-    def behind(j, pair, sub):
+    def behind(j, pair, sub, whole=True):
         qu, gu = stacked(q_v, j, pair, sub), stacked(g_v, j, pair, sub)
         rows = slice(sub * SUB, (sub + 1) * SUB)
         tops = [stats[sub, 0, c] for c in range(chunks)]
@@ -208,20 +292,25 @@
             w = p_ref[sub, at, :] * (factors[c][0:1] * inv)
             ds = (w * (dp_ref[sub, at, :] - delta)).astype(jnp.bfloat16)
             w = w.astype(jnp.bfloat16)
-            w_ref[sub, at, :] = w
-            ds_ref[sub, at, :] = ds
+            w_ref[pair * 2 + sub, at, :] = w
+            ds_ref[pair * 2 + sub, at, :] = ds
             if (c + 1) % BH == 0 or c + 1 == chunks:
                 low = c // BH * BH
                 wide = slice((sub + low) * SUB, (sub + c + 1) * SUB)
-                acc[0, wide, :] += dot(ds_ref[sub, low * SUB : (c + 1) * SUB, :], qu, NN)
-                acc[1, wide, :] += dot(w_ref[sub, low * SUB : (c + 1) * SUB, :], gu, NN)
+                acc[0, wide, :] += dot(ds_ref[pair * 2 + sub, low * SUB : (c + 1) * SUB, :], qu, NN)
+                acc[1, wide, :] += dot(w_ref[pair * 2 + sub, low * SUB : (c + 1) * SUB, :], gu, NN)
             yield
+        if whole:
+            yield from products(j, pair, sub)
+
+    def products(j, pair, sub):
+        rows = slice(sub * SUB, (sub + 1) * SUB)
         span = slice(sub * SUB, sub * SUB + WIN)
         for out, left, right, factor in (
             (att_ref, 1, w_ref, 1.0),
             (dq_ref, 0, ds_ref, scale),
         ):
-            product = dot(win_t[left, :, span], right[sub], NN)
+            product = dot(win_t[left, :, span], right[pair * 2 + sub], NN)
             for side in range(2):
                 at = pl.ds(pl.multiple_of(j * cols + (pair * 2 + side) * HEAD, HEAD), HEAD)
                 tile = product[:, side * SUB : (side + 1) * SUB]
@@ -237,61 +326,85 @@
     @pl.loop(0, KV_HEADS)
     def _(j):
         for which in range(2):
-            own_copy(j, which).wait()
             load(j, which).wait()
 
     arrive(0)
     for _ in ahead(0, 0, 0):
         pass
 
+    def head(j, final):
+        for which in range(2):
+            for r in range(0, W, SUB):
+                win_t[which, :, r : r + SUB] = win[
+                    j, r : r + SUB, which * HEAD : (which + 1) * HEAD
+                ].T
+        acc[...] = jnp.zeros_like(acc)
+
+        @pl.loop(0, pairs - 1)
+        def _(pair):
+            together(behind(j, pair, 0, not final), ahead(j, pair, 1), PATTERN)
+            together(behind(j, pair, 1, not final), ahead(j, pair + 1, 0), PATTERN)
+
+        if not final:
+
+            @pl.when(j + 2 < KV_HEADS)
+            def _():
+                start_shares(j + 2)
+
+            @pl.when(j + 3 < KV_HEADS)
+            def _():
+                start_cross(j + 3)
+
+        together(behind(j, pairs - 1, 0, not final), ahead(j, pairs - 1, 1), PATTERN)
+        if final:
+            for _ in behind(j, pairs - 1, 1, False):
+                pass
+        else:
+            arrive(j + 1)
+            together(behind(j, pairs - 1, 1), ahead(j + 1, 0, 0), PATTERN)
+        for which in range(2):
+            factor = scale if which == 0 else 1.0
+            out_part[which, j] = (acc[which, : W - T, :] * factor).astype(jnp.bfloat16)
+            each(lambda m: back(j, m, which).start())
+            own[which, j] = acc[which, W - T :, :] * factor
+
+    @pl.loop(0, KV_HEADS - 1)
+    def _(j):
+        @pl.when(j == 0)
+        def _():
+            start_shares(1)
+            start_cross(2)
+
+        head(j, False)
+
+        @pl.when(j > 0)
+        def _():
+            relay(j - 1)
+
+    final = KV_HEADS - 1
+    head(final, True)
+    relay(final - 1)
+
+    @pl.loop(0, pairs)
+    def _(pair):
+        for sub in range(2):
+            for _ in products(final, pair, sub):
+                pass
+
+    @pl.loop(0, KV_HEADS - 1)
+    def _(j):
+        finish(j)
+
+    relay(KV_HEADS - 1)
+    finish(KV_HEADS - 1)
+
     @pl.loop(0, KV_HEADS)
     def _(j):
-        @pl.when(j + 1 < KV_HEADS)
-        def _():
-            each(lambda d, which: send(j + 1, d, which).start())
-
-        for which in range(2):
-            for r in range(0, W, SUB):
-                win_t[which, :, r : r + SUB] = win[which, j, r : r + SUB, :].T
-        acc[...] = jnp.zeros_like(acc)
-
-        @pl.loop(0, pairs - 1)
-        def _(pair):
-            together(behind(j, pair, 0), ahead(j, pair, 1), PATTERN)
-            together(behind(j, pair, 1), ahead(j, pair + 1, 0), PATTERN)
-
-        together(behind(j, pairs - 1, 0), ahead(j, pairs - 1, 1), PATTERN)
-
-        @pl.when(j + 1 < KV_HEADS)
-        def _():
-            arrive(j + 1)
-            together(behind(j, pairs - 1, 1), ahead(j + 1, 0, 0), PATTERN)
-
-        @pl.when(j + 1 == KV_HEADS)
-        def _():
-            for _ in behind(j, pairs - 1, 1):
-                pass
-
-        for which in range(2):
-            factor = scale if which == 0 else 1.0
-            out_part[which, j] = (acc[which, : W - T, :] * factor).astype(jnp.bfloat16)
-            own[which, j] = acc[which, W - T :, :] * factor
-        each(lambda d, which: back(j, d, which).start())
-
-    @pl.loop(0, KV_HEADS)
-    def _(j):
-        each(lambda d, which: back(j, d, which).wait_recv())
-        at = pl.ds(pl.multiple_of(j * HEAD, HEAD), HEAD)
-        for which, ref in ((0, dk_ref), (1, dv_ref)):
-            sums = own[which, j]
-            for d in range(1, SPAN):
-                sums = sums + in_part[which, j, d - 1].astype(jnp.float32)
-            ref[:, at] = sums.astype(jnp.bfloat16)
-
-    @pl.loop(0, KV_HEADS)
-    def _(j):
-        each(lambda d, which: send(j, d, which).wait_send())
-        each(lambda d, which: back(j, d, which).wait_send())
+        each(lambda m: share(j, m, False).wait_send())
+        cross(j).wait_send()
+        for which in range(2):
+            each(lambda m: back(j, m, which).wait_send())
+            cross_back(j, which).wait_send()
 
 
 def place_results(*refs):
@@ -324,26 +437,33 @@
         scratch_shapes=[
             pltpu.VMEM((KV_HEADS, T, GROUP * HEAD), bf16),
             pltpu.VMEM((KV_HEADS, T, GROUP * HEAD), bf16),
-            pltpu.VMEM((2, KV_HEADS, W, HEAD), bf16),
+            pltpu.VMEM((2,) + keys.shape, bf16),
+            pltpu.VMEM((KV_HEADS, W + T, 2 * HEAD), bf16),
             pltpu.VMEM((2, HEAD, W), bf16),
             pltpu.VMEM((T // SUB, WIN, SUB), f32),
             pltpu.VMEM((2, WIN, 2 * SUB), f32),
             pltpu.VMEM((2, WIN, 2 * SUB), f32),
             pltpu.VMEM((2, 3, WIN // SUB, 8, 2 * SUB), f32),
-            pltpu.VMEM((2, WIN, 2 * SUB), bf16),
-            pltpu.VMEM((2, WIN, 2 * SUB), bf16),
+            pltpu.VMEM((GROUP, WIN, 2 * SUB), bf16),
+            pltpu.VMEM((GROUP, WIN, 2 * SUB), bf16),
             pltpu.VMEM((2, W, HEAD), f32),
             pltpu.VMEM((2, KV_HEADS, T, HEAD), f32),
             pltpu.VMEM((2, KV_HEADS, W - T, HEAD), bf16),
             pltpu.VMEM((2, KV_HEADS, SPAN - 1, T, HEAD), bf16),
+            pltpu.VMEM((2, KV_HEADS, T, HEAD), bf16),
+            pltpu.VMEM((2, KV_HEADS, T, HEAD), bf16),
             pltpu.SMEM(doc_lengths.shape, jnp.int32),
+            dma((KV_HEADS, 2)),
+            dma((2,)),
             dma(()),
+            dma((KV_HEADS,)),
+            dma((KV_HEADS,)),
+            dma((KV_HEADS, SPAN - 1)),
+            dma((KV_HEADS, SPAN - 1)),
+            dma((KV_HEADS, SPAN - 1, 2)),
+            dma((KV_HEADS, SPAN - 1, 2)),
             dma((KV_HEADS, 2)),
             dma((KV_HEADS, 2)),
-            dma((KV_HEADS, SPAN - 1, 2)),
-            dma((KV_HEADS, SPAN - 1, 2)),
-            dma((KV_HEADS, SPAN - 1, 2)),
-            dma((KV_HEADS, SPAN - 1, 2)),
         ],
         compiler_params=pltpu.CompilerParams(
             collective_id=0, has_side_effects=True, vmem_limit_bytes=48 * 1024 * 1024

time: 76.7 us -> 75 us (0.978); the launches traced: 75.2 us -> 74.9 us
  no operation moved by 1% of the time
where the time goes in v4:
time: 75 us; the launch traced here: 74.9 us
  Pallas kernels  74.3 us (99%)
    pallas_call x1, Pallas kernels, local(): pl.pallas_call(kernel, out_shape=(jax.ShapeDtypeStruct(queries.shape, bf1...  72.1 us
    pallas_call x1, Pallas kernels, local(): pl.pallas_call(place_results, out_shape=tuple((jax.ShapeDtypeStruct(x.sha...  2.2 us

profile of v4, /device:TPU:0, one launch (start us, length us, event | category | flops | bytes accessed | tf_op | source)
XLA Modules:
  0.0 74.9 jit_solution(6067063639479101127)
XLA Ops:
  0.6 72.1 %attention.1 = (bf16[256,4096]{1,0:T(8,128)(2,1)S(1)}, bf16[256,4096]{1,0:T(8,128)(2,1)S(1)}, bf16[256,512]{1,0:T(8,128)(2,1)S(1)}, bf16[256,512]{1,0:T(8,128)(2,1)S(1)}) custom-call(bf16[256,4096]{1,0:T(8,128)(2,1)} %q_hbm.1, bf16[256,512]{1,0:T(8,128)(2,1)} %k_hbm.1, bf16[256,512]{1,0:T(8,128)(2,1)} %v_hbm.1, bf16[256,4096]{1,0:T(8,128)(2,1)} %g_hbm.1, ...), custom_call_target="tpu_custom_call" | custom-call | tf_op jit(solution)/shard_map/attention/pallas_call | solution.py:427
  72.7 2.2 %results.1 = (bf16[256,4096]{1,0:T(8,128)(2,1)}, bf16[256,4096]{1,0:T(8,128)(2,1)}, bf16[256,512]{1,0:T(8,128)(2,1)}, bf16[256,512]{1,0:T(8,128)(2,1)}) custom-call(bf16[256,4096]{1,0:T(8,128)(2,1)S(1)} %get-tuple-element.8.refs_0_, bf16[256,4096]{1,0:T(8,128)(2,1)S(1)} %get-tuple-element.9.refs_1_, bf16[256,512]{1,0:T(8,128)(2,1)S(1)} %get-tuple-element.10.refs_2_, ...), custom_call_target="tpu_custom_call" | custom-call | tf_op jit(solution)/shard_map/results/pallas_call | solution.py:478

commit v5 on v4

--- a/solution.py
+++ b/solution.py
@@ -377,13 +377,13 @@
 
         head(j, False)
 
-        @pl.when(j > 0)
+        @pl.when(j > 1)
         def _():
-            relay(j - 1)
+            relay(j - 2)
 
     final = KV_HEADS - 1
     head(final, True)
-    relay(final - 1)
+    relay(final - 2)
 
     @pl.loop(0, pairs)
     def _(pair):
@@ -391,12 +391,12 @@
             for _ in products(final, pair, sub):
                 pass
 
-    @pl.loop(0, KV_HEADS - 1)
+    relay(final - 1)
+    relay(final)
+
+    @pl.loop(0, KV_HEADS)
     def _(j):
         finish(j)
-
-    relay(KV_HEADS - 1)
-    finish(KV_HEADS - 1)
 
     @pl.loop(0, KV_HEADS)
     def _(j):

time: 75 us -> 70.6 us (0.941)
  Pallas kernels: 74.3 us -> 69.9 us
    pallas_call x1, Pallas kernels: 72.1 us -> 67.7 us  [local(): pl.pallas_call(kernel, out_shape=(jax.ShapeDtypeStruct(queries.shape, bf1...]
where the time goes in v5:
time: 70.6 us; the launch traced here: 70.5 us
  Pallas kernels  69.9 us (99%)
    pallas_call x1, Pallas kernels, local(): pl.pallas_call(kernel, out_shape=(jax.ShapeDtypeStruct(queries.shape, bf1...  67.7 us
    pallas_call x1, Pallas kernels, local(): pl.pallas_call(place_results, out_shape=tuple((jax.ShapeDtypeStruct(x.sha...  2.2 us

profile of v5, /device:TPU:0, one launch (start us, length us, event | category | flops | bytes accessed | tf_op | source)
XLA Modules:
  0.0 70.5 jit_solution(7155925790839315276)
XLA Ops:
  0.6 67.7 %attention.1 = (bf16[256,4096]{1,0:T(8,128)(2,1)S(1)}, bf16[256,4096]{1,0:T(8,128)(2,1)S(1)}, bf16[256,512]{1,0:T(8,128)(2,1)S(1)}, bf16[256,512]{1,0:T(8,128)(2,1)S(1)}) custom-call(bf16[256,4096]{1,0:T(8,128)(2,1)} %q_hbm.1, bf16[256,512]{1,0:T(8,128)(2,1)} %k_hbm.1, bf16[256,512]{1,0:T(8,128)(2,1)} %v_hbm.1, bf16[256,4096]{1,0:T(8,128)(2,1)} %g_hbm.1, ...), custom_call_target="tpu_custom_call" | custom-call | tf_op jit(solution)/shard_map/attention/pallas_call | solution.py:427
  68.3 2.2 %results.1 = (bf16[256,4096]{1,0:T(8,128)(2,1)}, bf16[256,4096]{1,0:T(8,128)(2,1)}, bf16[256,512]{1,0:T(8,128)(2,1)}, bf16[256,512]{1,0:T(8,128)(2,1)}) custom-call(bf16[256,4096]{1,0:T(8,128)(2,1)S(1)} %get-tuple-element.8.refs_0_, bf16[256,4096]{1,0:T(8,128)(2,1)S(1)} %get-tuple-element.9.refs_1_, bf16[256,512]{1,0:T(8,128)(2,1)S(1)} %get-tuple-element.10.refs_2_, ...), custom_call_target="tpu_custom_call" | custom-call | tf_op jit(solution)/shard_map/results/pallas_call | solution.py:478

commit v6 on v5

--- a/solution.py
+++ b/solution.py
@@ -238,6 +238,7 @@
 
     start_relayed(0)
     start_cross(1)
+    start_cross(2)
     chunks = WIN // SUB
     to_exp2 = scale * math.log2(math.e)
 
@@ -351,10 +352,6 @@
             def _():
                 start_shares(j + 2)
 
-            @pl.when(j + 3 < KV_HEADS)
-            def _():
-                start_cross(j + 3)
-
         together(behind(j, pairs - 1, 0, not final), ahead(j, pairs - 1, 1), PATTERN)
         if final:
             for _ in behind(j, pairs - 1, 1, False):
@@ -373,7 +370,7 @@
         @pl.when(j == 0)
         def _():
             start_shares(1)
-            start_cross(2)
+            start_cross(3)
 
         head(j, False)
 

time: 70.6 us -> 70.6 us (level)
  no operation moved by 1% of the time
where the time goes in v6:
time: 70.6 us; the launch traced here: 70.5 us
  Pallas kernels  69.9 us (99%)
    pallas_call x1, Pallas kernels, local(): pl.pallas_call(kernel, out_shape=(jax.ShapeDtypeStruct(queries.shape, bf1...  67.7 us
    pallas_call x1, Pallas kernels, local(): pl.pallas_call(place_results, out_shape=tuple((jax.ShapeDtypeStruct(x.sha...  2.2 us

profile of v6, /device:TPU:0, one launch (start us, length us, event | category | flops | bytes accessed | tf_op | source)
XLA Modules:
  0.0 70.5 jit_solution(18183433054743505813)
XLA Ops:
  0.6 67.7 %attention.1 = (bf16[256,4096]{1,0:T(8,128)(2,1)S(1)}, bf16[256,4096]{1,0:T(8,128)(2,1)S(1)}, bf16[256,512]{1,0:T(8,128)(2,1)S(1)}, bf16[256,512]{1,0:T(8,128)(2,1)S(1)}) custom-call(bf16[256,4096]{1,0:T(8,128)(2,1)} %q_hbm.1, bf16[256,512]{1,0:T(8,128)(2,1)} %k_hbm.1, bf16[256,512]{1,0:T(8,128)(2,1)} %v_hbm.1, bf16[256,4096]{1,0:T(8,128)(2,1)} %g_hbm.1, ...), custom_call_target="tpu_custom_call" | custom-call | tf_op jit(solution)/shard_map/attention/pallas_call | solution.py:424
  68.3 2.2 %results.1 = (bf16[256,4096]{1,0:T(8,128)(2,1)}, bf16[256,4096]{1,0:T(8,128)(2,1)}, bf16[256,512]{1,0:T(8,128)(2,1)}, bf16[256,512]{1,0:T(8,128)(2,1)}) custom-call(bf16[256,4096]{1,0:T(8,128)(2,1)S(1)} %get-tuple-element.8.refs_0_, bf16[256,4096]{1,0:T(8,128)(2,1)S(1)} %get-tuple-element.9.refs_1_, bf16[256,512]{1,0:T(8,128)(2,1)S(1)} %get-tuple-element.10.refs_2_, ...), custom_call_target="tpu_custom_call" | custom-call | tf_op jit(solution)/shard_map/results/pallas_call | solution.py:475
